TPU v7x, 32 devices: a whole 2x2x4 slice. The times are simulated.
32 devices in a mesh: gene: 8 (over z, x), cell: 4 (over y, core).
Axes of the slice: x: 2, y: 2, z: 4, core: 2. Of those that a mesh axis runs over, the one named last changes fastest.
Arguments:
- gene_tokens: bfloat16 [16, 4096, 768], P('cell', 'gene')
- latents: bfloat16 [64, 768], replicated, may hold values from -6 to 6
- head_temp: float32 [12], replicated, may hold values from 1.5 to 4
- w_key: bfloat16 [768, 768], replicated, may hold values from -0.21875 to 0.21875
- w_value: bfloat16 [768, 768], replicated, may hold values from -0.21875 to 0.21875
- w_out: bfloat16 [768, 768], replicated, may hold values from -0.21875 to 0.21875
- w_set_qkv: bfloat16 [768, 2304], replicated, may hold values from -0.21875 to 0.21875
- w_set_out: bfloat16 [768, 768], replicated, may hold values from -0.21875 to 0.21875
- set_ids: int32 [16], P('cell'), may hold values from 0 to 7, as said below
Outputs:
- latent_states: bfloat16 [16, 64, 768], P('cell', 'gene')
- set_states: bfloat16 [16, 768], P('cell')
Inputs may be any that keep to these rules, and one draw needn't show every extreme that they name: `set_ids`: set s is held by index s mod 4 of cell. At most 2 cells of one device's block belong to sets held by one index, and in every draw one index holds the sets of exactly 2 cells of every device's block.
All inputs are finite; a program needn't handle non-finite values.
Results may differ from a plain program's by a relative error of at most 0.012.
Values may be sent and summed in bfloat16 or wider, within the bound.
A program may use at most 64 MiB of HBM per device.

v0:
```python
import math
import jax
import jax.numpy as jnp
from jax import lax
from jax.sharding import PartitionSpec as P

EPSILON = 1e-06


def head_norm(array, head_count):
    shaped = array.reshape(array.shape[:-1] + (head_count, array.shape[-1] // head_count))
    return shaped * lax.rsqrt(jnp.mean(shaped * shaped, axis=-1, keepdims=True) + EPSILON)


def set_project(inputs, w_set_qkv, head_count):
    model_width = inputs.shape[1]
    head_size = model_width // head_count
    projected = jnp.dot(inputs, w_set_qkv, preferred_element_type=jnp.float32)
    queries = (head_norm(projected[:, :model_width], head_count) / math.sqrt(head_size)).astype(
        jnp.bfloat16
    )
    key_rows = head_norm(projected[:, model_width : 2 * model_width], head_count).astype(
        jnp.bfloat16
    )
    value_rows = (
        projected[:, 2 * model_width :]
        .reshape(inputs.shape[0], head_count, head_size)
        .astype(jnp.bfloat16)
    )
    return (queries, key_rows, value_rows)


def set_attend(queries, key_rows, value_rows, query_ids, key_ids, residual, w_set_out):
    scores = jnp.einsum("qhe,khe->hqk", queries, key_rows, preferred_element_type=jnp.float32)
    matching = query_ids[:, None] == key_ids[None, :]
    weights = jnp.where(matching[None], jnp.exp(scores), 0.0)
    totals = jnp.sum(weights, axis=2)
    numerator = jnp.einsum(
        "hqk,khe->qhe", weights.astype(jnp.bfloat16), value_rows, preferred_element_type=jnp.float32
    )
    attended = (
        (numerator / jnp.transpose(totals)[:, :, None])
        .reshape(queries.shape[0], -1)
        .astype(jnp.bfloat16)
    )
    return (
        residual.astype(jnp.float32)
        + jnp.dot(attended, w_set_out, preferred_element_type=jnp.float32)
    ).astype(jnp.bfloat16)


def on_device(
    gene_tokens, latents, head_temp, w_key, w_value, w_out, w_set_qkv, w_set_out, set_ids
):
    cell_count, gene_count, model_width = gene_tokens.shape
    latent_count = latents.shape[0]
    head_count = head_temp.shape[0]
    head_size = model_width // head_count
    queries = (
        head_norm(latents.astype(jnp.float32), head_count)
        * (head_temp[:, None] / math.sqrt(head_size))
    ).astype(jnp.bfloat16)
    key_rows = head_norm(
        jnp.einsum("cgd,de->cge", gene_tokens, w_key, preferred_element_type=jnp.float32),
        head_count,
    ).astype(jnp.bfloat16)
    value_rows = jnp.einsum(
        "cgd,de->cge", gene_tokens, w_value, preferred_element_type=jnp.float32
    ).astype(jnp.bfloat16)
    value_rows = value_rows.reshape(cell_count, gene_count, head_count, head_size)
    scores = jnp.einsum("lhe,cghe->chlg", queries, key_rows, preferred_element_type=jnp.float32)
    weights = jnp.exp(scores)
    totals = jnp.transpose(jnp.sum(weights, axis=3), (0, 2, 1))
    numerator = jnp.einsum(
        "chlg,cghe->clhe",
        weights.astype(jnp.bfloat16),
        value_rows,
        preferred_element_type=jnp.float32,
    )
    numerator = numerator.reshape(cell_count, latent_count, model_width)
    numerator, totals = (
        lax.psum(numerator.astype(jnp.bfloat16), "gene").astype(jnp.float32),
        lax.psum(totals.astype(jnp.bfloat16), "gene").astype(jnp.float32),
    )
    portion = latent_count // lax.axis_size("gene")
    first_row = lax.axis_index("gene") * portion
    attended = (
        numerator.reshape(cell_count, latent_count, head_count, head_size) / totals[..., None]
    )
    attended = attended.reshape(cell_count, latent_count, model_width).astype(jnp.bfloat16)
    mixed_rows = latents.astype(jnp.float32)[None] + jnp.einsum(
        "cld,de->cle", attended, w_out, preferred_element_type=jnp.float32
    )
    pooled = jnp.mean(mixed_rows, axis=1)
    latent_states = lax.dynamic_slice_in_dim(mixed_rows, first_row, portion, 1).astype(jnp.bfloat16)
    set_input = (
        pooled * lax.rsqrt(jnp.mean(pooled * pooled, axis=1, keepdims=True) + EPSILON)
    ).astype(jnp.bfloat16)
    every_input, every_ids = (
        lax.all_gather(set_input, "cell", axis=0, tiled=True),
        lax.all_gather(set_ids, "cell", axis=0, tiled=True),
    )
    set_queries, set_keys, set_values = set_project(every_input, w_set_qkv, head_count)
    own_queries = lax.dynamic_slice_in_dim(
        set_queries, lax.axis_index("cell") * cell_count, cell_count, 0
    )
    set_states = set_attend(
        own_queries, set_keys, set_values, set_ids, every_ids, set_input, w_set_out
    )
    return (latent_states, set_states)


def solution(mesh):
    in_specs = (P("cell", "gene", None), P(), P(), P(), P(), P(), P(), P(), P("cell"))
    out_specs = (P("cell", "gene", None), P("cell", None))
    return jax.shard_map(
        on_device, mesh=mesh, in_specs=in_specs, out_specs=out_specs, check_vma=False
    )
```

profile of v0, /device:TPU:0, one launch (start us, length us, event | category | flops | bytes accessed | tf_op | source)
XLA Modules:
  0.0 154.6 jit_solution(15478738839907730430)
XLA Ops:
  7.2 2.0 %reshape.103 = f32[64,12,64]{2,1,0:T(8,128)} reshape(bf16[64,768]{1,0:T(8,128)(2,1)} %param.10) | data formatting | bytes 294912 | tf_op jit(solution)/shard_map/reshape | solution.py:11
  9.2 1.3 multiply_reduce_fusion.1
  10.5 0.6 add_rsqrt_fusion.1
  11.1 0.7 broadcast_multiply_fusion
  11.8 5.0 %fusion.8 = f32[4,512,768]{1,2,0:T(8,128)S(1)} fusion(bf16[4,512,768]{2,1,0:T(8,128)(2,1)} %param.9, bf16[768,768]{1,0:T(8,128)(2,1)} %param.12), kind=kOutput, calls=%fused_computation.12 | convolution fusion | flops 2415919104 | bytes 10616832 | tf_op jit(solution)/shard_map/cgd,de->cge/dot_general | solution.py:64
  16.8 1.0 multiply_reduce_fusion
  17.8 2.2 %copy-done.1 = f32[4,512,768]{1,2,0:T(8,128)} copy-done((f32[4,512,768]{1,2,0:T(8,128)}, f32[4,512,768]{1,2,0:T(8,128)S(1)}, u32[]{:S(2)}) %copy-start.1) | copy-done | bytes 6291480
  20.0 0.7 add_rsqrt_fusion
  20.7 0.3 copy-done.3
  21.0 0.4 copy-done.4
  21.4 4.0 %convolution_convert_fusion = bf16[4,512,768]{2,1,0:T(8,128)(2,1)} fusion(bf16[4,512,768]{2,1,0:T(8,128)(2,1)S(1)} %copy-done.3, bf16[768,768]{1,0:T(8,128)(2,1)S(1)} %copy-done.4), kind=kOutput, calls=%fused_computation.8 | convolution fusion | flops 2417491968 | bytes 7471104 | tf_op jit(solution)/shard_map/cgd,de->cge/dot_general | solution.py:67
  25.3 4.7 %copy.30 = bf16[4,512,768]{1,2,0:T(8,128)(2,1)} copy(bf16[4,512,768]{2,1,0:T(8,128)(2,1)} %convolution_convert_fusion) | data formatting | bytes 6291456 | tf_op jit(solution)/shard_map/convert_element_type | solution.py:69
  30.1 1.2 fusion.15
  31.4 4.8 %bitcast_reduce_fusion = (bf16[4,12,64]{2,0,1:T(4,128)(2,1)}, f32[12,4,512,64]{2,3,1,0:T(8,128)S(1)}) fusion(bf16[64,12,64,1]{2,1,0,3:T(8,128)(2,1)S(1)} %fusion.15, f32[4,512,12,64]{1,3,2,0:T(8,128)} %bitcast.45, f32[4,512,12]{1,2,0:T(8,128)} %add_rsqrt_fusion), kind=kOutput, calls=%fused_computation | convolution fusion | flops 206042112 | bytes 12785664 | tf_op jit(solution)/shard_map/lhe,cghe->chlg/dot_general | solution.py:71
  36.1 1.9 %fusion.4 = bf16[4,12,64,64]{3,2,1,0:T(8,128)(2,1)} fusion(bf16[4,512,12,64]{1,3,2,0:T(8,128)(2,1)S(1)} %bitcast.46, f32[12,4,512,64]{2,3,1,0:T(8,128)S(1)} %get-tuple-element.5), kind=kOutput, calls=%fused_computation.9 | convolution fusion | flops 203096064 | bytes 9830400 | tf_op jit(solution)/shard_map/chlg,cghe->clhe/dot_general | solution.py:74
  38.0 2.1 %copy.35 = bf16[4,64,768]{2,1,0:T(8,128)(2,1)} copy(bf16[4,64,768]{1,2,0:T(8,128)(2,1)} %bitcast.47) | data formatting | bytes 786432 | tf_op jit(solution)/shard_map/convert_element_type | solution.py:82
  40.2 1.6 %convert_element_type.71 = f32[64,768]{1,0:T(8,128)} convert(bf16[64,768]{1,0:T(8,128)(2,1)} %param.10) | non-fusion elementwise | flops 49152 | bytes 294912 | tf_op jit(solution)/shard_map/convert_element_type | solution.py:91
  41.8 38.9 %psum.15 = bf16[4,64,12]{1,0,2:T(4,128)(2,1)S(1)} all-reduce(bf16[4,64,12]{1,0,2:T(4,128)(2,1)} %bitcast.48), channel_id=1, replica_groups=mesh['gene'=8,'cell'=4] {'gene'}, use_global_device_ids=true, to_apply=%region_4.0 | all-reduce | flops 3072 | bytes 12288 | tf_op jit(solution)/shard_map/psum | solution.py:83
  80.7 0.8 copy.36
  81.5 2.9 %div.60 = f32[4,64,12,64]{3,2,1,0:T(8,128)} broadcast(f32[4,64,12]{2,1,0:T(8,128)} %copy.36), dimensions={0,1,2} | broadcast | bytes 798720 | tf_op jit(solution)/shard_map/div | solution.py:88
  84.4 2.7 %div.61 = f32[4,64,768]{2,1,0:T(8,128)} reshape(f32[4,64,12,64]{3,2,1,0:T(8,128)} %div.60) | data formatting | bytes 1572864 | tf_op jit(solution)/shard_map/div | solution.py:88
  87.1 1.2 dynamic-slice
  89.0 0.2 dynamic-update-slice
  89.2 4.9 %all-reduce = s32[16]{0:T(128)S(1)} all-reduce(s32[16]{0:T(128)S(1)} %dynamic-update-slice), channel_id=1, replica_groups=mesh['gene'=8,'cell'=4] {'cell'}, use_global_device_ids=true, to_apply=%add | all-reduce | flops 16 | bytes 128
  94.2 0.6 broadcast_compare_fusion
  94.8 19.7 %all-reduce.3.cloned.1.call-done = bf16[4,64,768]{2,1,0:T(8,128)(2,1)} async-done(((bf16[4,64,768]{2,1,0:T(8,128)(2,1)}), bf16[4,64,768]{2,1,0:T(8,128)(2,1)}) %all-reduce.3.cloned.1.call-update) | async-done | bytes 393232 | tf_op jit(solution)/shard_map/psum | solution.py:82
  114.5 2.9 %fusion.28 = (f32[4,768]{1,0:T(4,128)S(1)}, bf16[4,64,768]{2,1,0:T(8,128)(2,1)}) fusion(bf16[768,768]{1,0:T(8,128)(2,1)} %param.14, f32[4,64,768]{2,1,0:T(8,128)} %div.61, bf16[4,64,768]{2,1,0:T(8,128)(2,1)} %all-reduce.3.cloned.1.call-done, f32[64,768]{1,0:T(8,128)} %convert_element_type.71), kind=kOutput, calls=%fused_computation.55 | convolution fusion | flops 303166464 | bytes 2961408 | tf_op jit(solution)/shard_map/cld,de->cle/dot_general | solution.py:91
  117.5 5.6 %all-gather = bf16[4,4,768]{2,1,0:T(4,128)(2,1)} all-gather(bf16[1,4,768]{2,1,0:T(4,128)(2,1)S(1)} %fusion.26), channel_id=1, replica_groups=mesh['gene'=8,'cell'=4] {'cell'}, dimensions={0}, use_global_device_ids=true | all-gather | bytes 30720 | tf_op jit(solution)/shard_map/all_gather | solution.py:100
  123.2 1.4 reshape.110
  124.5 1.3 fusion.30
  125.9 0.7 fusion.27
  126.5 0.6 slice.17
  127.1 1.5 reshape.105
  128.6 1.0 multiply_reduce_fusion.2
  129.7 1.6 %multiply_convert_fusion.2 = bf16[16,12,64]{2,1,0:T(8,128)(2,1)} fusion(f32[16,12,64]{2,1,0:T(8,128)} %reshape.105, f32[16,12]{1,0:T(8,128)S(1)} %add_rsqrt_fusion.2), kind=kLoop, calls=%fused_computation.27 | loop fusion | flops 24576 | bytes 74496 | tf_op jit(solution)/shard_map/convert_element_type | solution.py:22
  131.3 1.5 reshape.104
  132.8 1.0 multiply_reduce_fusion.3
  133.8 1.4 constant_dynamic-slice_fusion
  135.2 0.6 add_rsqrt_fusion.3
  135.8 1.4 copy.37
  137.2 1.4 constant_dynamic-slice_fusion.1
  138.6 1.5 convert_element_type.87
  140.0 1.2 fusion.29
  141.2 1.0 fusion.13
  142.2 0.6 copy.41
  142.8 1.4 convert_element_type.92
  144.2 2.2 %fusion.14 = bf16[4,768]{1,0:T(4,128)(2,1)} fusion(bf16[4,768]{1,0:T(4,128)(2,1)} %convert_element_type.92, bf16[768,768]{1,0:T(8,128)(2,1)} %param.16, f32[4,768]{1,0:T(4,128)S(1)} %get-tuple-element.6, f32[4]{0:T(128)S(1)} %rsqrt_multiply_fusion), kind=kOutput, calls=%fused_computation.21 | convolution fusion | flops 4733952 | bytes 1204240 | tf_op jit(solution)/shard_map/dot_general | solution.py:48
  146.3 1.4 dynamic-slice_convert_fusion
  (16 shorter events, 0.3 us)
Async XLA Ops:
  7.2 117.4 %copy-start = (bf16[768,2304]{1,0:T(8,128)(2,1)S(1)}, bf16[768,2304]{1,0:T(8,128)(2,1)}, u32[]{:S(2)}) copy-start(bf16[768,2304]{1,0:T(8,128)(2,1)} %param.15) | copy-start | bytes 10616836
  7.2 107.3 %all-reduce.3.cloned.1.call-start = ((), (), s32[]{:S(2)}) async-start(), calls=%async_computation | async-start | bytes 786432 | tf_op jit(solution)/shard_map/psum | solution.py:82
  16.8 3.2 %copy-start.1 = (f32[4,512,768]{1,2,0:T(8,128)}, f32[4,512,768]{1,2,0:T(8,128)S(1)}, u32[]{:S(2)}) copy-start(f32[4,512,768]{1,2,0:T(8,128)S(1)} %fusion.8) | copy-start | bytes 18874372
  16.8 4.2 %copy-start.3 = (bf16[4,512,768]{2,1,0:T(8,128)(2,1)S(1)}, bf16[4,512,768]{2,1,0:T(8,128)(2,1)}, u32[]{:S(2)}) copy-start(bf16[4,512,768]{2,1,0:T(8,128)(2,1)} %param.9) | copy-start | bytes 9437188
  16.8 4.5 %copy-start.4 = (bf16[768,768]{1,0:T(8,128)(2,1)S(1)}, bf16[768,768]{1,0:T(8,128)(2,1)}, u32[]{:S(2)}) copy-start(bf16[768,768]{1,0:T(8,128)(2,1)} %param.13) | copy-start | bytes 3538948
  31.3 4.8 %copy-start.2 = (bf16[4,512,768]{1,2,0:T(8,128)(2,1)S(1)}, bf16[4,512,768]{1,2,0:T(8,128)(2,1)}, u32[]{:S(2)}) copy-start(bf16[4,512,768]{1,2,0:T(8,128)(2,1)} %copy.30) | copy-start | bytes 9437188
  40.2 48.8 %copy-start.5 = (s32[4]{0:T(128)S(1)}, s32[4]{0:T(128)}, u32[]{:S(2)}) copy-start(s32[4]{0:T(128)} %param.17) | copy-start | bytes 52
Sparse Core Ops, SparseCore 0:
  40.3 74.0 all-reduce.2
where the time goes:
time: 156 us; the launch traced here: 155 us
  blocking collectives  49.5 us (32%)
  local copies, waits for them, and re-layouts  34.3 us (22%)
  matrix products  24.2 us (16%)
  waiting for transfers between devices  19.7 us (13%)
  between operations  14.8 us (9%)
  other arithmetic  12.1 us (8%)
    psum x1, blocking collectives, on_device(): lax.psum(totals.astype(jnp.bfloat16), 'gene').astype(jnp.float32)  38.9 us
    psum x1, waiting for transfers between devices, on_device(): lax.psum(numerator.astype(jnp.bfloat16), 'gene').astype(jnp.float32)  19.7 us
    unnamed x16, local copies, waits for them, and re-layouts  5.73 us
    all_gather x1, blocking collectives, on_device(): lax.all_gather(set_input, 'cell', axis=0, tiled=True)  5.63 us
    div x2, local copies, waits for them, and re-layouts, on_device(): numerator.reshape(cell_count, latent_count, head_count, head_size)  5.58 us
    reshape x3, local copies, waits for them, and re-layouts, head_norm(): array.reshape(array.shape[:-1] + (head_count, array.shape[-1] // head_cou...  5.07 us
    dot_general x1, matrix products, on_device(): jnp.einsum('cgd,de->cge', gene_tokens, w_key, preferred_element_type=jnp....  5.02 us
    unnamed x1, blocking collectives  4.93 us
  transfers between devices with their start and end apart: 1, of which 1 were waited for; matrix products, arithmetic and copies ran while one was open for 6% of the time, Pallas kernels for 0%

commit v1 on v0

--- a/solution.py
+++ b/solution.py
@@ -79,7 +79,7 @@
     )
     numerator = numerator.reshape(cell_count, latent_count, model_width)
     numerator, totals = (
-        lax.psum(numerator.astype(jnp.bfloat16), "gene").astype(jnp.float32),
+        jnp.sum(lax.all_gather(numerator.astype(jnp.bfloat16), "gene"), axis=0).astype(jnp.float32),
         lax.psum(totals.astype(jnp.bfloat16), "gene").astype(jnp.float32),
     )
     portion = latent_count // lax.axis_size("gene")

time: 156 us -> 148 us (0.949)
  waiting for transfers between devices: 19.7 us -> 8.68 us
  other arithmetic: 12.1 us -> 15.2 us
    psum x1 -> x0, waiting for transfers between devices: 19.7 us -> none  [on_device(): lax.psum(numerator.astype(jnp.bfloat16), 'gene').astype(jnp.float32)]
    all_gather x0 -> x1, waiting for transfers between devices: none -> 8.66 us  [on_device(): lax.all_gather(numerator.astype(jnp.bfloat16), 'gene')]
    reduce_sum x0 -> x1, other arithmetic: none -> 3.17 us  [on_device(): jnp.sum(lax.all_gather(numerator.astype(jnp.bfloat16), 'gene'), axis=0)]
  transfers between devices with their start and end apart: 1 -> 1, of which waited for: 1 -> 1; matrix products, arithmetic and copies ran while one was open for 6% -> 7% of each run, Pallas kernels for 0% -> 0%
where the time goes in v1:
time: 148 us; the launch traced here: 147 us
  blocking collectives  49.8 us (34%)
  local copies, waits for them, and re-layouts  34.3 us (23%)
  matrix products  24.2 us (16%)
  other arithmetic  15.2 us (10%)
  between operations  14.8 us (10%)
  waiting for transfers between devices  8.68 us (6%)
    psum x1, blocking collectives, on_device(): lax.psum(totals.astype(jnp.bfloat16), 'gene').astype(jnp.float32)  39.3 us
    all_gather x1, waiting for transfers between devices, on_device(): lax.all_gather(numerator.astype(jnp.bfloat16), 'gene')  8.66 us
    unnamed x16, local copies, waits for them, and re-layouts  5.73 us
    all_gather x1, blocking collectives, on_device(): lax.all_gather(set_input, 'cell', axis=0, tiled=True)  5.63 us
    div x2, local copies, waits for them, and re-layouts, on_device(): numerator.reshape(cell_count, latent_count, head_count, head_size)  5.6 us
    reshape x3, local copies, waits for them, and re-layouts, head_norm(): array.reshape(array.shape[:-1] + (head_count, array.shape[-1] // head_cou...  5.07 us
    dot_general x1, matrix products, on_device(): jnp.einsum('cgd,de->cge', gene_tokens, w_key, preferred_element_type=jnp....  5.02 us
    unnamed x1, blocking collectives  4.85 us
  transfers between devices with their start and end apart: 1, of which 1 were waited for; matrix products, arithmetic and copies ran while one was open for 7% of the time, Pallas kernels for 0%

profile of v1, /device:TPU:0, one launch (start us, length us, event | category | flops | bytes accessed | tf_op | source)
XLA Modules:
  0.0 147.0 jit_solution(15994579717606464118)
XLA Ops:
  7.2 2.0 %reshape.114 = f32[64,12,64]{2,1,0:T(8,128)} reshape(bf16[64,768]{1,0:T(8,128)(2,1)} %param.10) | data formatting | bytes 294912 | tf_op jit(solution)/shard_map/reshape | solution.py:11
  9.2 1.3 multiply_reduce_fusion.1
  10.5 0.6 add_rsqrt_fusion.1
  11.1 0.7 broadcast_multiply_fusion
  11.8 5.0 %fusion.8 = f32[4,512,768]{1,2,0:T(8,128)S(1)} fusion(bf16[4,512,768]{2,1,0:T(8,128)(2,1)} %param.9, bf16[768,768]{1,0:T(8,128)(2,1)} %param.12), kind=kOutput, calls=%fused_computation.12 | convolution fusion | flops 2415919104 | bytes 10616832 | tf_op jit(solution)/shard_map/cgd,de->cge/dot_general | solution.py:64
  16.8 1.0 multiply_reduce_fusion
  17.8 2.2 %copy-done.1 = f32[4,512,768]{1,2,0:T(8,128)} copy-done((f32[4,512,768]{1,2,0:T(8,128)}, f32[4,512,768]{1,2,0:T(8,128)S(1)}, u32[]{:S(2)}) %copy-start.1) | copy-done | bytes 6291480
  20.0 0.7 add_rsqrt_fusion
  20.7 0.3 copy-done.3
  21.0 0.4 copy-done.4
  21.4 4.0 %convolution_convert_fusion = bf16[4,512,768]{2,1,0:T(8,128)(2,1)} fusion(bf16[4,512,768]{2,1,0:T(8,128)(2,1)S(1)} %copy-done.3, bf16[768,768]{1,0:T(8,128)(2,1)S(1)} %copy-done.4), kind=kOutput, calls=%fused_computation.8 | convolution fusion | flops 2417491968 | bytes 7471104 | tf_op jit(solution)/shard_map/cgd,de->cge/dot_general | solution.py:67
  25.3 4.7 %copy.43 = bf16[4,512,768]{1,2,0:T(8,128)(2,1)} copy(bf16[4,512,768]{2,1,0:T(8,128)(2,1)} %convolution_convert_fusion) | data formatting | bytes 6291456 | tf_op jit(solution)/shard_map/convert_element_type | solution.py:69
  30.1 1.2 fusion.15
  31.4 4.8 %bitcast_reduce_fusion = (bf16[4,12,64]{2,0,1:T(4,128)(2,1)}, f32[12,4,512,64]{2,3,1,0:T(8,128)S(1)}) fusion(bf16[64,12,64,1]{2,1,0,3:T(8,128)(2,1)S(1)} %fusion.15, f32[4,512,12,64]{1,3,2,0:T(8,128)} %bitcast.45, f32[4,512,12]{1,2,0:T(8,128)} %add_rsqrt_fusion), kind=kOutput, calls=%fused_computation | convolution fusion | flops 206042112 | bytes 12785664 | tf_op jit(solution)/shard_map/lhe,cghe->chlg/dot_general | solution.py:71
  36.1 1.9 %fusion.4 = bf16[4,12,64,64]{3,2,1,0:T(8,128)(2,1)} fusion(bf16[4,512,12,64]{1,3,2,0:T(8,128)(2,1)S(1)} %bitcast.46, f32[12,4,512,64]{2,3,1,0:T(8,128)S(1)} %get-tuple-element.5), kind=kOutput, calls=%fused_computation.9 | convolution fusion | flops 203096064 | bytes 9830400 | tf_op jit(solution)/shard_map/chlg,cghe->clhe/dot_general | solution.py:74
  38.0 2.1 %copy.48 = bf16[1,4,64,768]{3,2,1,0:T(8,128)(2,1)} copy(bf16[1,4,64,768]{2,3,1,0:T(8,128)(2,1)} %bitcast.47) | data formatting | bytes 786432 | tf_op jit(solution)/shard_map/convert_element_type | solution.py:82
  40.2 1.6 %convert_element_type.82 = f32[64,768]{1,0:T(8,128)} convert(bf16[64,768]{1,0:T(8,128)(2,1)} %param.10) | non-fusion elementwise | flops 49152 | bytes 294912 | tf_op jit(solution)/shard_map/convert_element_type | solution.py:91
  41.8 39.3 %psum.7 = bf16[4,64,12]{1,0,2:T(4,128)(2,1)S(1)} all-reduce(bf16[4,64,12]{1,0,2:T(4,128)(2,1)} %bitcast.48), channel_id=1, replica_groups=mesh['gene'=8,'cell'=4] {'gene'}, use_global_device_ids=true, to_apply=%region_4.0 | all-reduce | flops 3072 | bytes 12288 | tf_op jit(solution)/shard_map/psum | solution.py:83
  81.1 0.8 copy.51
  81.8 2.9 %div.60 = f32[4,64,12,64]{3,2,1,0:T(8,128)} broadcast(f32[4,64,12]{2,1,0:T(8,128)} %copy.51), dimensions={0,1,2} | broadcast | bytes 798720 | tf_op jit(solution)/shard_map/div | solution.py:88
  84.7 2.7 %div.61 = f32[4,64,768]{2,1,0:T(8,128)} reshape(f32[4,64,12,64]{3,2,1,0:T(8,128)} %div.60) | data formatting | bytes 1572864 | tf_op jit(solution)/shard_map/div | solution.py:88
  87.5 1.2 dynamic-slice
  89.6 4.9 %all-reduce = s32[16]{0:T(128)S(1)} all-reduce(s32[16]{0:T(128)S(1)} %dynamic-update-slice), channel_id=1, replica_groups=mesh['gene'=8,'cell'=4] {'cell'}, use_global_device_ids=true, to_apply=%add | all-reduce | flops 16 | bytes 128
  94.5 0.6 broadcast_compare_fusion
  95.0 8.7 %all-gather.3.cloned.1.call-done = bf16[8,4,64,768]{3,2,1,0:T(8,128)(2,1)} async-done(((bf16[1,4,64,768]{3,2,1,0:T(8,128)(2,1)}), bf16[8,4,64,768]{3,2,1,0:T(8,128)(2,1)}) %all-gather.3.cloned.1.call-update) | async-done | bytes 3145744 | tf_op jit(solution)/shard_map/all_gather | solution.py:82
  103.7 3.2 %reduce_sum.86 = bf16[4,64,768]{2,1,0:T(8,128)(2,1)} reduce(bf16[8,4,64,768]{3,2,1,0:T(8,128)(2,1)} %all-gather.3.cloned.1.call-done, bf16[]{:T(256)} %constant.18.clone.1), dimensions={0}, to_apply=%region_2.0 | reduce | flops 1376256 | bytes 3538946 | tf_op jit(solution)/shard_map/reduce_sum | solution.py:82
  106.9 2.9 %fusion.28 = (f32[4,768]{1,0:T(4,128)S(1)}, bf16[4,64,768]{2,1,0:T(8,128)(2,1)}) fusion(bf16[768,768]{1,0:T(8,128)(2,1)} %param.14, f32[4,64,768]{2,1,0:T(8,128)} %div.61, bf16[4,64,768]{2,1,0:T(8,128)(2,1)} %reduce_sum.86, f32[64,768]{1,0:T(8,128)} %convert_element_type.82), kind=kOutput, calls=%fused_computation.55 | convolution fusion | flops 303166464 | bytes 2961408 | tf_op jit(solution)/shard_map/cld,de->cle/dot_general | solution.py:91
  110.0 5.6 %all-gather = bf16[4,4,768]{2,1,0:T(4,128)(2,1)} all-gather(bf16[1,4,768]{2,1,0:T(4,128)(2,1)S(1)} %fusion.26), channel_id=1, replica_groups=mesh['gene'=8,'cell'=4] {'cell'}, dimensions={0}, use_global_device_ids=true | all-gather | bytes 30720 | tf_op jit(solution)/shard_map/all_gather | solution.py:100
  115.6 1.4 reshape.121
  117.0 1.3 fusion.30
  118.3 0.7 fusion.27
  118.9 0.6 slice.17
  119.5 1.5 %reshape.116 = f32[16,12,64]{2,1,0:T(8,128)} reshape(f32[16,768]{1,0:T(8,128)} %get-tuple-element.3) | data formatting | bytes 98304 | tf_op jit(solution)/shard_map/reshape | solution.py:11
  121.1 1.0 multiply_reduce_fusion.2
  122.1 1.6 %multiply_convert_fusion.2 = bf16[16,12,64]{2,1,0:T(8,128)(2,1)} fusion(f32[16,12,64]{2,1,0:T(8,128)} %reshape.116, f32[16,12]{1,0:T(8,128)S(1)} %add_rsqrt_fusion.2), kind=kLoop, calls=%fused_computation.27 | loop fusion | flops 24576 | bytes 74496 | tf_op jit(solution)/shard_map/convert_element_type | solution.py:22
  123.7 1.5 %reshape.115 = f32[16,12,64]{2,1,0:T(8,128)} reshape(f32[16,768]{1,0:T(8,128)} %get-tuple-element.2) | data formatting | bytes 98304 | tf_op jit(solution)/shard_map/reshape | solution.py:11
  125.2 1.0 multiply_reduce_fusion.3
  126.3 1.4 constant_dynamic-slice_fusion
  127.6 0.6 add_rsqrt_fusion.3
  128.2 1.4 copy.52
  129.6 1.4 constant_dynamic-slice_fusion.1
  131.0 1.5 convert_element_type.98
  132.4 1.2 fusion.29
  133.6 1.0 fusion.13
  134.6 0.6 copy.56
  135.2 1.4 convert_element_type.103
  136.6 2.2 %fusion.14 = bf16[4,768]{1,0:T(4,128)(2,1)} fusion(bf16[4,768]{1,0:T(4,128)(2,1)} %convert_element_type.103, bf16[768,768]{1,0:T(8,128)(2,1)} %param.16, f32[4,768]{1,0:T(4,128)S(1)} %get-tuple-element.6, f32[4]{0:T(128)S(1)} %rsqrt_multiply_fusion), kind=kOutput, calls=%fused_computation.21 | convolution fusion | flops 4733952 | bytes 1204240 | tf_op jit(solution)/shard_map/dot_general | solution.py:48
  138.7 1.4 dynamic-slice_convert_fusion
  (17 shorter events, 0.5 us)
Async XLA Ops:
  7.2 109.8 %copy-start = (bf16[768,2304]{1,0:T(8,128)(2,1)S(1)}, bf16[768,2304]{1,0:T(8,128)(2,1)}, u32[]{:S(2)}) copy-start(bf16[768,2304]{1,0:T(8,128)(2,1)} %param.15) | copy-start | bytes 10616836
  7.2 96.5 %all-gather.3.cloned.1.call-start = ((), (), s32[]{:S(2)}) async-start(), calls=%async_computation | async-start | bytes 3538944 | tf_op jit(solution)/shard_map/all_gather | solution.py:82
  16.8 3.2 %copy-start.1 = (f32[4,512,768]{1,2,0:T(8,128)}, f32[4,512,768]{1,2,0:T(8,128)S(1)}, u32[]{:S(2)}) copy-start(f32[4,512,768]{1,2,0:T(8,128)S(1)} %fusion.8) | copy-start | bytes 18874372
  16.8 4.2 %copy-start.3 = (bf16[4,512,768]{2,1,0:T(8,128)(2,1)S(1)}, bf16[4,512,768]{2,1,0:T(8,128)(2,1)}, u32[]{:S(2)}) copy-start(bf16[4,512,768]{2,1,0:T(8,128)(2,1)} %param.9) | copy-start | bytes 9437188
  16.8 4.5 %copy-start.4 = (bf16[768,768]{1,0:T(8,128)(2,1)S(1)}, bf16[768,768]{1,0:T(8,128)(2,1)}, u32[]{:S(2)}) copy-start(bf16[768,768]{1,0:T(8,128)(2,1)} %param.13) | copy-start | bytes 3538948
  31.3 4.8 %copy-start.2 = (bf16[4,512,768]{1,2,0:T(8,128)(2,1)S(1)}, bf16[4,512,768]{1,2,0:T(8,128)(2,1)}, u32[]{:S(2)}) copy-start(bf16[4,512,768]{1,2,0:T(8,128)(2,1)} %copy.43) | copy-start | bytes 9437188
  40.2 49.2 %copy-start.5 = (s32[4]{0:T(128)S(1)}, s32[4]{0:T(128)}, u32[]{:S(2)}) copy-start(s32[4]{0:T(128)} %param.17) | copy-start | bytes 52
Sparse Core Ops, SparseCore 0:
  40.3 63.3 all-gather.2
